TPU v7x, 32 devices: a whole 2x2x4 slice. The times are simulated.
32 devices in a mesh: groups: 2 (over y), tok: 16 (over z, x, core).
Axes of the slice: x: 2, y: 2, z: 4, core: 2. Of those that a mesh axis runs over, the one named last changes fastest.
Arguments:
- queries: bfloat16 [1024, 2048], P(('groups', 'tok')), parts along dimension 0, may hold values from -6 to 6
- new_kv: bfloat16 [3072, 4096], P(('groups', 'tok')), parts along dimension 0, may hold values from -6 to 6
- prev_kv: bfloat16 [2, 3072, 4096], P(None, ('groups', 'tok')), parts along dimension 1, may hold values from -6 to 6
- base_step: int32 [32], P(('groups', 'tok')), parts along dimension 0, may hold values from 0 to 1
- live_counts: int32 [32], P('groups'), parts along dimension 0, may hold values from 1 to 96
- sketch: float32 [4096, 32], replicated, may hold values from -0.09375 to 0.09375
- cache: bfloat16 [64, 1536, 128], P(('groups', 'tok')), parts along dimension 0, may hold values from -6 to 6, as said below
- w_out: bfloat16 [2048, 1536], replicated, may hold values from -0.125 to 0.125
Outputs:
- projected: bfloat16 [1024, 1536], P(('groups', 'tok')), parts along dimension 0
There are 2 independent parts, one for each index of `groups`. A program takes and returns all parts, laid end to end along the dimension named above; an argument that names none is the same for every part. Nothing has to cross between parts.
Inputs may be any that keep to these rules, and one draw needn't show every extreme that they name: cache slots i and j hold the same values when i // 2 == j // 2 and i % 2 == j % 2.
All inputs are finite; a program needn't handle non-finite values.
Results may differ from a plain program's by a relative error of at most 0.019.
Values may be sent and summed in bfloat16 or wider, within the bound.
No kernel may reach another device: no remote copies, remote signals or barrier semaphores. Data moves between devices by JAX's collectives and lax.ppermute only.
A program may use at most 128 MiB of HBM per device.

v0:
```python
import math
import jax
import jax.numpy as jnp
from jax import lax
from jax.sharding import PartitionSpec as P

HD = 64
SWEEPS = 2
highest = lax.Precision.HIGHEST


def orthonormal(block_cols):
    gram_matrix = jnp.dot(block_cols.T, block_cols, precision=highest)
    lower_factor = jnp.linalg.cholesky(gram_matrix)
    return jax.scipy.linalg.solve_triangular(lower_factor, block_cols.T, lower=True).T


def compress(delta_block, sketch):
    basis_cols = orthonormal(jnp.dot(delta_block, sketch, precision=highest))
    for sweep_index in range(SWEEPS):
        inner = jnp.dot(delta_block.T, basis_cols, precision=highest)
        basis_cols = orthonormal(jnp.dot(delta_block, inner, precision=highest))
    right_factor = jnp.dot(basis_cols.T, delta_block, precision=highest)
    return (basis_cols.astype(jnp.bfloat16), right_factor.astype(jnp.bfloat16))


def spread_heads(matrix, head_groups, groups_q, width):
    lead = matrix.shape[0]
    per_group = matrix.reshape(lead, head_groups, width).transpose(1, 0, 2)
    copies = jnp.broadcast_to(per_group[:, None], (head_groups, groups_q, lead, width))
    return copies.reshape(head_groups * groups_q, lead, width)


def attend_head(pieces, live_keys):
    q_head, keys_values = pieces
    key_part = keys_values[:, :HD]
    value_part = keys_values[:, HD:]
    query_count = q_head.shape[0]
    block_rows = math.gcd(query_count, 512)

    def one_block(query_block):
        scores = jnp.dot(query_block, key_part.T, preferred_element_type=jnp.float32) * HD ** (-0.5)
        scores = jnp.where(live_keys[None, :], scores, -1e30)
        row_max = jnp.max(scores, axis=-1, keepdims=True)
        exponent = jnp.exp(scores - row_max)
        weights = (exponent / jnp.sum(exponent, axis=-1, keepdims=True)).astype(jnp.bfloat16)
        return jnp.dot(weights, value_part, preferred_element_type=jnp.float32).astype(jnp.bfloat16)

    return lax.map(one_block, q_head.reshape(query_count // block_rows, block_rows, HD)).reshape(
        query_count, HD
    )


def per_device(queries, new_kv, prev_kv, base_step, live_counts, sketch, cache, w_out):
    shards = lax.axis_size("tok")
    tok_rows = new_kv.shape[0]
    query_rows = queries.shape[0]
    head_count = queries.shape[1] // HD
    groups_q = max(1, shards // head_count)
    per_dev = head_count * groups_q // shards
    head_groups = head_count // per_dev
    part_rows = query_rows // groups_q
    width = per_dev * 2 * HD
    key_count = shards * tok_rows
    query_count = shards * part_rows
    prior = prev_kv[0].astype(jnp.float32)
    prior = jnp.where(base_step[0] == 1, prev_kv[1].astype(jnp.float32), prior)
    delta = new_kv.astype(jnp.float32) - prior
    left_factor, right_factor = compress(delta, sketch)
    rank_cols = left_factor.shape[1]
    q_blocks = queries.reshape(groups_q, part_rows, head_groups, per_dev * HD)
    q_blocks = q_blocks.transpose(2, 0, 1, 3).reshape(shards, part_rows, per_dev * HD)
    w_blocks = spread_heads(right_factor, head_groups, groups_q, width)
    q_here = lax.all_to_all(q_blocks, "tok", split_axis=0, concat_axis=0, tiled=True)
    u_here = lax.all_gather(left_factor, "tok", axis=0, tiled=True).reshape(
        shards, tok_rows, rank_cols
    )
    w_here = lax.all_to_all(w_blocks, "tok", split_axis=0, concat_axis=0, tiled=True)
    lowrank = jnp.einsum("str,src->stc", u_here, w_here, preferred_element_type=jnp.float32).astype(
        jnp.bfloat16
    )
    lowrank = lowrank.reshape(key_count, per_dev, 2 * HD).transpose(1, 0, 2)
    keys_values = (cache.astype(jnp.float32) + lowrank.astype(jnp.float32)).astype(jnp.bfloat16)
    live_keys = (jnp.arange(tok_rows, dtype=jnp.int32)[None, :] < live_counts[:, None]).reshape(
        key_count
    )
    q_heads = q_here.reshape(query_count, per_dev, HD).transpose(1, 0, 2)
    attended = lax.map(lambda pieces: attend_head(pieces, live_keys), (q_heads, keys_values))
    attended = attended.transpose(1, 0, 2).reshape(shards, part_rows, per_dev * HD)
    returned = lax.all_to_all(attended, "tok", split_axis=0, concat_axis=0, tiled=True)
    returned = returned.reshape(head_groups, groups_q, part_rows, per_dev * HD)
    row_block = returned.transpose(1, 2, 0, 3).reshape(query_rows, head_count * HD)
    return jnp.dot(row_block, w_out, preferred_element_type=jnp.float32).astype(jnp.bfloat16)


def solution(mesh):
    return jax.shard_map(
        per_device,
        mesh=mesh,
        in_specs=(
            P(("groups", "tok"), None),
            P(("groups", "tok"), None),
            P(None, ("groups", "tok"), None),
            P(("groups", "tok")),
            P("groups"),
            P(),
            P(("groups", "tok"), None, None),
            P(),
        ),
        out_specs=P(("groups", "tok"), None),
        check_vma=False,
    )
```

profile of v0, /device:TPU:0, one launch (start us, length us, event | category | flops | bytes accessed | tf_op | source)
XLA Modules:
  0.0 94.7 jit_solution(8483638808945009714)
XLA Ops:
  0.0 0.0 copy-start
  0.0 1.0 %copy.33 = bf16[4,8,16,128]{3,2,1,0:T(8,128)(2,1)S(1)} copy(bf16[4,8,16,128]{3,1,2,0:T(8,128)(2,1)} %bitcast.116) | data formatting | bytes 262144
  1.0 0.7 copy.43
  1.7 7.4 %all-to-all-start = ((bf16[16,32,128]{2,1,0:T(8,128)(2,1)}), bf16[16,32,128]{2,1,0:T(8,128)(2,1)S(1)}, u32[]{:S(2)}, u32[]{:S(2)}) async-start(bf16[16,32,128]{2,1,0:T(8,128)(2,1)} %bitcast.103), calls=%async_computation | async-start | bytes 262144 | tf_op jit(solution)/shard_map/all_to_all | solution.py:74
  9.7 1.9 %bitcast_subtract_fusion = f32[96,4096]{1,0:T(8,128)S(1)} fusion(bf16[96,4096]{1,0:T(8,128)(2,1)} %param.14, bf16[2,96,4096]{2,1,0:T(8,128)(2,1)} %param.15, pred[]{:T(512)} %bitcast.3), kind=kLoop, calls=%fused_computation.21 | loop fusion | flops 1966080 | bytes 3932161 | tf_op jit(solution)/shard_map/sub | solution.py:68
  11.6 0.0 copy-done
  11.6 1.3 %fusion.37 = f32[96,32]{0,1:T(8,128)S(1)} fusion(f32[96,4096]{1,0:T(8,128)S(1)} %bitcast_subtract_fusion, f32[4096,32]{0,1:T(8,128)S(1)} %copy-done), kind=kOutput, calls=%fused_computation.61 | convolution fusion | flops 150994944 | bytes 2109440 | tf_op jit(solution)/shard_map/dot_general | solution.py:19
  13.0 0.1 fusion.38
  13.1 0.1 copy.24
  13.2 2.9 %cholesky.59 = f32[32,32]{1,0:T(8,128)S(1)} custom-call(f32[32,32]{1,0:T(8,128)S(1)} %fusion.31), custom_call_target="Cholesky" | custom-call | tf_op jit(solution)/shard_map/jit(cholesky)/cholesky | solution.py:14
  16.2 0.6 compare_reduce_fusion.2
  16.8 0.7 fusion.17
  17.5 2.4 %custom-call.7 = f32[1,32,32]{1,2,0:T(8,128)S(1)} custom-call(f32[1,32,32]{2,1,0:T(8,128)S(1)} %fusion.17), custom_call_target="InvertDiagBlocksLowerTriangular" | custom-call | tf_op jit(solution)/shard_map/jit(_solve_triangular)/triangular_solve | solution.py:15
  19.9 0.2 fusion.28
  20.1 1.0 %fusion.39 = f32[4096,32]{0,1:T(8,128)S(1)} fusion(f32[96,4096]{1,0:T(8,128)S(1)} %bitcast_subtract_fusion, f32[32,96]{1,0:T(8,128)S(1)} %fusion.28), kind=kOutput, calls=%fused_computation.63 | convolution fusion | flops 150994944 | bytes 2109440 | tf_op jit(solution)/shard_map/dot_general | solution.py:21
  21.2 1.3 %fusion.40 = f32[96,32]{0,1:T(8,128)S(1)} fusion(f32[96,4096]{1,0:T(8,128)S(1)} %bitcast_subtract_fusion, f32[4096,32]{0,1:T(8,128)S(1)} %fusion.39), kind=kOutput, calls=%fused_computation.64 | convolution fusion | flops 150994944 | bytes 2109440 | tf_op jit(solution)/shard_map/dot_general | solution.py:22
  22.5 0.1 fusion.41
  22.7 0.1 copy.25
  22.7 2.9 %cholesky.70 = f32[32,32]{1,0:T(8,128)S(1)} custom-call(f32[32,32]{1,0:T(8,128)S(1)} %fusion.27), custom_call_target="Cholesky" | custom-call | tf_op jit(solution)/shard_map/jit(cholesky)/cholesky | solution.py:14
  25.7 0.6 compare_reduce_fusion.1
  26.3 0.7 fusion.18
  27.0 2.4 %custom-call.8 = f32[1,32,32]{1,2,0:T(8,128)S(1)} custom-call(f32[1,32,32]{2,1,0:T(8,128)S(1)} %fusion.18), custom_call_target="InvertDiagBlocksLowerTriangular" | custom-call | tf_op jit(solution)/shard_map/jit(_solve_triangular)/triangular_solve | solution.py:15
  29.4 0.2 fusion.24
  29.7 1.0 %fusion.42 = f32[4096,32]{0,1:T(8,128)S(1)} fusion(f32[96,4096]{1,0:T(8,128)S(1)} %bitcast_subtract_fusion, f32[32,96]{1,0:T(8,128)S(1)} %fusion.24), kind=kOutput, calls=%fused_computation.66 | convolution fusion | flops 150994944 | bytes 2109440 | tf_op jit(solution)/shard_map/dot_general | solution.py:21
  30.7 1.3 %fusion.43 = f32[96,32]{0,1:T(8,128)S(1)} fusion(f32[96,4096]{1,0:T(8,128)S(1)} %bitcast_subtract_fusion, f32[4096,32]{0,1:T(8,128)S(1)} %fusion.42), kind=kOutput, calls=%fused_computation.67 | convolution fusion | flops 150994944 | bytes 2109440 | tf_op jit(solution)/shard_map/dot_general | solution.py:22
  32.0 0.1 fusion.44
  32.2 0.1 copy.26
  32.3 2.9 %cholesky.81 = f32[32,32]{1,0:T(8,128)S(1)} custom-call(f32[32,32]{1,0:T(8,128)S(1)} %fusion.23), custom_call_target="Cholesky" | custom-call | tf_op jit(solution)/shard_map/jit(cholesky)/cholesky | solution.py:14
  35.2 0.6 compare_reduce_fusion
  35.9 0.7 fusion.19
  36.5 2.4 %custom-call.9 = f32[1,32,32]{1,2,0:T(8,128)S(1)} custom-call(f32[1,32,32]{2,1,0:T(8,128)S(1)} %fusion.19), custom_call_target="InvertDiagBlocksLowerTriangular" | custom-call | tf_op jit(solution)/shard_map/jit(_solve_triangular)/triangular_solve | solution.py:15
  39.0 0.2 fusion.20
  39.2 0.9 convolution_convert_fusion
  40.1 0.7 copy.42
  40.8 0.0 all-to-all-done
  40.8 6.0 %all-to-all-start.1 = ((bf16[16,32,256]{2,1,0:T(8,128)(2,1)}), bf16[16,32,256]{2,1,0:T(8,128)(2,1)S(1)}, u32[]{:S(2)}, u32[]{:S(2)}) async-start(bf16[16,32,256]{2,1,0:T(8,128)(2,1)} %bitcast.102), calls=%async_computation.1 | async-start | bytes 524288 | tf_op jit(solution)/shard_map/all_to_all | solution.py:78
  46.8 22.3 %all-gather = bf16[16,96,32]{1,2,0:T(8,128)(2,1)S(1)} all-gather(bf16[1,96,32]{1,2,0:T(8,128)(2,1)S(1)} %convert_bitcast_fusion), channel_id=1, replica_groups=mesh['groups'=2,'tok'=16] {'tok'}, dimensions={0}, use_global_device_ids=true | all-gather | bytes 104448 | tf_op jit(solution)/shard_map/all_gather | solution.py:75
  69.2 0.1 reshape.49
  69.4 0.0 all-to-all-done.1
  69.4 1.6 %fusion.14 = f32[16,96,256]{2,1,0:T(8,128)} fusion(bf16[16,96,32]{1,2,0:T(8,128)(2,1)S(1)} %all-gather, bf16[16,32,256]{2,1,0:T(8,128)(2,1)S(1)} %all-to-all-done.1), kind=kOutput, calls=%fused_computation.23 | convolution fusion | flops 25952256 | bytes 1933312 | tf_op jit(solution)/shard_map/str,src->stc/dot_general | solution.py:79
  71.0 2.1 %reshape.55 = f32[1536,2,128]{2,1,0:T(2,128)S(1)} reshape(f32[16,96,256]{2,1,0:T(8,128)} %fusion.14) | data formatting | bytes 3145728 | tf_op jit(solution)/shard_map/convert_element_type | solution.py:83
  73.0 0.0 copy-start.1
  73.0 1.3 %fusion.13 = bf16[2,1536,128]{2,1,0:T(8,128)(2,1)S(1)} fusion(f32[1536,2,128]{2,1,0:T(2,128)S(1)} %reshape.55, bf16[2,1536,128]{2,1,0:T(8,128)(2,1)} %param.19), kind=kLoop, calls=%fused_computation.20 | loop fusion | flops 1179648 | bytes 3145728 | tf_op jit(solution)/shard_map/convert_element_type | solution.py:83
  74.3 0.0 copy-done.1
  74.3 4.9 %while.11 = (s32[]{:T(128)}, bf16[2,512,64]{1,2,0:T(8,128)(2,1)S(1)}, bf16[2,512,64]{2,1,0:T(8,128)(2,1)S(1)}, bf16[2,1536,128]{2,1,0:T(8,128)(2,1)S(1)}, s32[16]{0:T(128)S(1)}, /*index=5*/s32[]{:T(128)}) while((s32[]{:T(128)}, bf16[2,512,64]{1,2,0:T(8,128)(2,1)S(1)}, bf16[2,512,64]{2,1,0:T(8,128)(2,1)S(1)}, ...), condition=%wide.region_5.8_spmd.clone, body=%wide.region_2.7_spmd.clone.sunk | while | flops 207651328 | bytes 11223697 | solution.py:88
  74.4 0.1 iota_compare_fusion.4
  74.5 0.1 broadcast_in_dim.43
  74.5 0.7 fusion.71
  75.2 0.6 fusion.72
  75.8 1.0 %fusion.73 = bf16[2,512,64]{1,2,0:T(8,128)(2,1)S(1)} fusion(bf16[2,512,64]{1,2,0:T(8,128)(2,1)S(1)} %get-tuple-element.130, s32[]{:T(128)} %get-tuple-element.129, f32[512,1536]{1,0:T(8,128)S(1)} %get-tuple-element.121, f32[512]{0:T(512)S(1)} %fusion.72, f32[512]{0:T(512)S(1)} %get-tuple-element.122, ...), kind=kOutput, calls=%fused_computation.9.clone.1 | convolution fusion | flops 103055360 | bytes 3608580 | tf_op jit(solution)/shard_map/while/body/eval_jaxpr/while/body/eval_jaxpr/dot_general | solution.py:47
  76.8 0.1 iota_compare_fusion.4
  76.9 0.1 broadcast_in_dim.43
  77.0 0.7 fusion.71
  77.7 0.6 fusion.72
  78.3 1.0 %fusion.73 = bf16[2,512,64]{1,2,0:T(8,128)(2,1)S(1)} fusion(bf16[2,512,64]{1,2,0:T(8,128)(2,1)S(1)} %get-tuple-element.130, s32[]{:T(128)} %get-tuple-element.129, f32[512,1536]{1,0:T(8,128)S(1)} %get-tuple-element.121, f32[512]{0:T(512)S(1)} %fusion.72, f32[512]{0:T(512)S(1)} %get-tuple-element.122, ...), kind=kOutput, calls=%fused_computation.9.clone.1 | convolution fusion | flops 103055360 | bytes 3608580 | tf_op jit(solution)/shard_map/while/body/eval_jaxpr/while/body/eval_jaxpr/dot_general | solution.py:47
  79.3 0.2 copy.30
  79.4 0.1 reshape.52
  79.6 10.5 %all_to_all.15 = bf16[16,32,128]{2,1,0:T(8,128)(2,1)S(1)} all-to-all(bf16[16,32,128]{2,1,0:T(8,128)(2,1)S(1)} %reshape.52), channel_id=1, replica_groups=mesh['groups'=2,'tok'=16] {'tok'}, dimensions={0} | all-to-all | bytes 262144 | tf_op jit(solution)/shard_map/all_to_all | solution.py:90
  90.1 0.1 copy.31
  90.1 4.6 %convolution_convert_fusion.1 = bf16[32,1536]{1,0:T(8,128)(2,1)} fusion(bf16[2048,1536]{1,0:T(8,128)(2,1)} %param.20, bf16[4,8,16,128]{3,2,1,0:T(8,128)(2,1)S(1)} %bitcast.112), kind=kOutput, calls=%fused_computation.18 | convolution fusion | flops 201375744 | bytes 6520832 | tf_op jit(solution)/shard_map/dot_general | solution.py:93
  (11 shorter events, 0.2 us)
Async XLA Ops:
  0.0 11.6 %copy-start = (f32[4096,32]{0,1:T(8,128)S(1)}, f32[4096,32]{0,1:T(8,128)}, u32[]{:S(2)}) copy-start(f32[4096,32]{0,1:T(8,128)} %param.18) | copy-start | bytes 1572868
  1.7 39.1 %all-to-all-start = ((bf16[16,32,128]{2,1,0:T(8,128)(2,1)}), bf16[16,32,128]{2,1,0:T(8,128)(2,1)S(1)}, u32[]{:S(2)}, u32[]{:S(2)}) async-start(bf16[16,32,128]{2,1,0:T(8,128)(2,1)} %bitcast.103), calls=%async_computation | async-start | bytes 262144 | tf_op jit(solution)/shard_map/all_to_all | solution.py:74
  40.8 28.6 %all-to-all-start.1 = ((bf16[16,32,256]{2,1,0:T(8,128)(2,1)}), bf16[16,32,256]{2,1,0:T(8,128)(2,1)S(1)}, u32[]{:S(2)}, u32[]{:S(2)}) async-start(bf16[16,32,256]{2,1,0:T(8,128)(2,1)} %bitcast.102), calls=%async_computation.1 | async-start | bytes 524288 | tf_op jit(solution)/shard_map/all_to_all | solution.py:78
  73.0 1.3 %copy-start.1 = (s32[16]{0:T(128)S(1)}, s32[16]{0:T(128)}, u32[]{:S(2)}) copy-start(s32[16]{0:T(128)} %param.17) | copy-start | bytes 196
where the time goes:
time: 95.2 us; the launch traced here: 94.7 us
  blocking collectives  32.8 us (34%)
  other arithmetic  24.6 us (26%)
  matrix products  17.5 us (18%)
  starting transfers between devices  13.4 us (14%)
  local copies, waits for them, and re-layouts  5.45 us (6%)
    all_gather x1, blocking collectives, per_device(): lax.all_gather(left_factor, 'tok', axis=0, tiled=True)  22.3 us
    another operation x9, other arithmetic, orthonormal(): lower_factor = jnp.linalg.cholesky(gram_matrix)  10.8 us
    all_to_all x1, blocking collectives, per_device(): lax.all_to_all(attended, 'tok', split_axis=0, concat_axis=0, tiled=True)  10.5 us
    another operation x6, other arithmetic, orthonormal(): jax.scipy.linalg.solve_triangular(lower_factor, block_cols.T, lower=True)  9.26 us
    all_to_all x1, starting transfers between devices, per_device(): lax.all_to_all(q_blocks, 'tok', split_axis=0, concat_axis=0, tiled=True)  7.39 us
    all_to_all x1, starting transfers between devices, per_device(): lax.all_to_all(w_blocks, 'tok', split_axis=0, concat_axis=0, tiled=True)  6.01 us
    dot_general x1, matrix products, per_device(): jnp.dot(row_block, w_out, preferred_element_type=jnp.float32)  4.56 us
    dot_general x2, matrix products, compress(): basis_cols = orthonormal(jnp.dot(delta_block, inner, precision=highest))  2.69 us
  transfers between devices with their start and end apart: 2, of which 0 were waited for; matrix products, arithmetic and copies ran while one was open for 33% of the time, Pallas kernels for 0%

commit v1 on v0

--- a/solution.py
+++ b/solution.py
@@ -87,7 +87,18 @@
     q_heads = q_here.reshape(query_count, per_dev, HD).transpose(1, 0, 2)
     attended = lax.map(lambda pieces: attend_head(pieces, live_keys), (q_heads, keys_values))
     attended = attended.transpose(1, 0, 2).reshape(shards, part_rows, per_dev * HD)
-    returned = lax.all_to_all(attended, "tok", split_axis=0, concat_axis=0, tiled=True)
+    ways, here = (lax.axis_size("tok"), lax.axis_index("tok"))
+    width_2 = attended.shape[0] // ways
+    dims = list(attended.shape)
+    dims[0] = width_2
+    height = dims[0]
+    dims[0] = height * ways
+    returned = jnp.zeros(dims, attended.dtype)
+    for mask in range(ways):
+        part = lax.dynamic_slice_in_dim(attended, (here ^ mask) * width_2, width_2, axis=0)
+        if mask:
+            part = lax.ppermute(part, "tok", [(d, d ^ mask) for d in range(ways)])
+        returned = lax.dynamic_update_slice_in_dim(returned, part, (here ^ mask) * height, axis=0)
     returned = returned.reshape(head_groups, groups_q, part_rows, per_dev * HD)
     row_block = returned.transpose(1, 2, 0, 3).reshape(query_rows, head_count * HD)
     return jnp.dot(row_block, w_out, preferred_element_type=jnp.float32).astype(jnp.bfloat16)

time: 95.2 us -> 109 us (1.14)
  starting transfers between devices: 13.4 us -> 33.7 us
  blocking collectives: 32.8 us -> 22.3 us
  waiting for transfers between devices: 0.01 us -> 1.86 us
  local copies, waits for them, and re-layouts: 5.45 us -> 7.18 us
    ppermute x0 -> x15, starting transfers between devices: none -> 20.3 us  [per_device(): part = lax.ppermute(part, 'tok', [(d, d ^ mask) for d in range(ways)])]
    all_to_all x1 -> x0, blocking collectives: 10.5 us -> none  [per_device(): lax.all_to_all(attended, 'tok', split_axis=0, concat_axis=0, tiled=True)]
    ppermute x0 -> x15, waiting for transfers between devices: none -> 1.86 us  [per_device(): part = lax.ppermute(part, 'tok', [(d, d ^ mask) for d in range(ways)])]
    dynamic_update_slice x0 -> x16, local copies, waits for them, and re-layouts: none -> 1.45 us  [per_device(): lax.dynamic_update_slice_in_dim(returned, part, (here ^ mask) * height, a...]
  transfers between devices with their start and end apart: 2 -> 17, of which waited for: 0 -> 2; matrix products, arithmetic and copies ran while one was open for 33% -> 29% of each run, Pallas kernels for 0% -> 0%
where the time goes in v1:
time: 109 us; the launch traced here: 108 us
  starting transfers between devices  33.7 us (31%)
  other arithmetic  24.6 us (23%)
  blocking collectives  22.3 us (20%)
  matrix products  17.5 us (16%)
  local copies, waits for them, and re-layouts  7.18 us (7%)
  waiting for transfers between devices  1.86 us (2%)
  between operations  1.25 us (1%)
    all_gather x1, blocking collectives, per_device(): lax.all_gather(left_factor, 'tok', axis=0, tiled=True)  22.3 us
    ppermute x15, starting transfers between devices, per_device(): part = lax.ppermute(part, 'tok', [(d, d ^ mask) for d in range(ways)])  20.3 us
    another operation x9, other arithmetic, orthonormal(): lower_factor = jnp.linalg.cholesky(gram_matrix)  10.8 us
    another operation x6, other arithmetic, orthonormal(): jax.scipy.linalg.solve_triangular(lower_factor, block_cols.T, lower=True)  9.26 us
    all_to_all x1, starting transfers between devices, per_device(): lax.all_to_all(q_blocks, 'tok', split_axis=0, concat_axis=0, tiled=True)  7.39 us
    all_to_all x1, starting transfers between devices, per_device(): lax.all_to_all(w_blocks, 'tok', split_axis=0, concat_axis=0, tiled=True)  6.01 us
    dot_general x1, matrix products, per_device(): jnp.dot(row_block, w_out, preferred_element_type=jnp.float32)  4.56 us
    dot_general x2, matrix products, compress(): basis_cols = orthonormal(jnp.dot(delta_block, inner, precision=highest))  2.69 us
  transfers between devices with their start and end apart: 17, of which 2 were waited for; matrix products, arithmetic and copies ran while one was open for 29% of the time, Pallas kernels for 0%

profile of v1, /device:TPU:0, one launch (start us, length us, event | category | flops | bytes accessed | tf_op | source)
XLA Modules:
  0.0 108.5 jit_solution(15240968153499442122)
XLA Ops:
  0.0 1.0 copy.71
  1.0 0.7 copy.81
  1.7 7.4 %all-to-all-start = ((bf16[16,32,128]{2,1,0:T(8,128)(2,1)}), bf16[16,32,128]{2,1,0:T(8,128)(2,1)S(1)}, u32[]{:S(2)}, u32[]{:S(2)}) async-start(bf16[16,32,128]{2,1,0:T(8,128)(2,1)} %bitcast.118), calls=%async_computation | async-start | bytes 262144 | tf_op jit(solution)/shard_map/all_to_all | solution.py:74
  9.7 1.9 %bitcast_subtract_fusion = f32[96,4096]{1,0:T(8,128)S(1)} fusion(bf16[96,4096]{1,0:T(8,128)(2,1)} %param.14, bf16[2,96,4096]{2,1,0:T(8,128)(2,1)} %param.15, pred[]{:T(512)} %bitcast.3), kind=kLoop, calls=%fused_computation.21 | loop fusion | flops 1966080 | bytes 3932161 | tf_op jit(solution)/shard_map/sub | solution.py:68
  11.6 1.3 %fusion.37 = f32[96,32]{0,1:T(8,128)S(1)} fusion(f32[96,4096]{1,0:T(8,128)S(1)} %bitcast_subtract_fusion, f32[4096,32]{0,1:T(8,128)S(1)} %copy-done), kind=kOutput, calls=%fused_computation.77 | convolution fusion | flops 150994944 | bytes 2109440 | tf_op jit(solution)/shard_map/dot_general | solution.py:19
  13.0 0.1 fusion.38
  13.2 2.9 %cholesky.59 = f32[32,32]{1,0:T(8,128)S(1)} custom-call(f32[32,32]{1,0:T(8,128)S(1)} %fusion.31), custom_call_target="Cholesky" | custom-call | tf_op jit(solution)/shard_map/jit(cholesky)/cholesky | solution.py:14
  16.2 0.6 compare_reduce_fusion.2
  16.8 0.7 fusion.17
  17.5 2.4 %custom-call.7 = f32[1,32,32]{1,2,0:T(8,128)S(1)} custom-call(f32[1,32,32]{2,1,0:T(8,128)S(1)} %fusion.17), custom_call_target="InvertDiagBlocksLowerTriangular" | custom-call | tf_op jit(solution)/shard_map/jit(_solve_triangular)/triangular_solve | solution.py:15
  19.9 0.2 fusion.28
  20.1 1.0 fusion.39
  21.2 1.3 %fusion.40 = f32[96,32]{0,1:T(8,128)S(1)} fusion(f32[96,4096]{1,0:T(8,128)S(1)} %bitcast_subtract_fusion, f32[4096,32]{0,1:T(8,128)S(1)} %fusion.39), kind=kOutput, calls=%fused_computation.80 | convolution fusion | flops 150994944 | bytes 2109440 | tf_op jit(solution)/shard_map/dot_general | solution.py:22
  22.5 0.1 fusion.41
  22.7 2.9 %cholesky.70 = f32[32,32]{1,0:T(8,128)S(1)} custom-call(f32[32,32]{1,0:T(8,128)S(1)} %fusion.27), custom_call_target="Cholesky" | custom-call | tf_op jit(solution)/shard_map/jit(cholesky)/cholesky | solution.py:14
  25.7 0.6 compare_reduce_fusion.1
  26.3 0.7 fusion.18
  27.0 2.4 %custom-call.8 = f32[1,32,32]{1,2,0:T(8,128)S(1)} custom-call(f32[1,32,32]{2,1,0:T(8,128)S(1)} %fusion.18), custom_call_target="InvertDiagBlocksLowerTriangular" | custom-call | tf_op jit(solution)/shard_map/jit(_solve_triangular)/triangular_solve | solution.py:15
  29.4 0.2 fusion.24
  29.7 1.0 fusion.42
  30.7 1.3 %fusion.43 = f32[96,32]{0,1:T(8,128)S(1)} fusion(f32[96,4096]{1,0:T(8,128)S(1)} %bitcast_subtract_fusion, f32[4096,32]{0,1:T(8,128)S(1)} %fusion.42), kind=kOutput, calls=%fused_computation.83 | convolution fusion | flops 150994944 | bytes 2109440 | tf_op jit(solution)/shard_map/dot_general | solution.py:22
  32.0 0.1 fusion.44
  32.3 2.9 %cholesky.81 = f32[32,32]{1,0:T(8,128)S(1)} custom-call(f32[32,32]{1,0:T(8,128)S(1)} %fusion.23), custom_call_target="Cholesky" | custom-call | tf_op jit(solution)/shard_map/jit(cholesky)/cholesky | solution.py:14
  35.2 0.6 compare_reduce_fusion
  35.9 0.7 fusion.19
  36.5 2.4 %custom-call.9 = f32[1,32,32]{1,2,0:T(8,128)S(1)} custom-call(f32[1,32,32]{2,1,0:T(8,128)S(1)} %fusion.19), custom_call_target="InvertDiagBlocksLowerTriangular" | custom-call | tf_op jit(solution)/shard_map/jit(_solve_triangular)/triangular_solve | solution.py:15
  39.0 0.2 fusion.20
  39.2 0.9 convolution_convert_fusion
  40.1 0.7 copy.80
  40.8 6.0 %all-to-all-start.1 = ((bf16[16,32,256]{2,1,0:T(8,128)(2,1)}), bf16[16,32,256]{2,1,0:T(8,128)(2,1)S(1)}, u32[]{:S(2)}, u32[]{:S(2)}) async-start(bf16[16,32,256]{2,1,0:T(8,128)(2,1)} %bitcast.117), calls=%async_computation.1 | async-start | bytes 524288 | tf_op jit(solution)/shard_map/all_to_all | solution.py:78
  46.9 22.3 %all-gather = bf16[16,96,32]{1,2,0:T(8,128)(2,1)S(1)} all-gather(bf16[1,96,32]{1,2,0:T(8,128)(2,1)S(1)} %convert_bitcast_fusion), channel_id=1, replica_groups=mesh['groups'=2,'tok'=16] {'tok'}, dimensions={0}, use_global_device_ids=true | all-gather | bytes 104448 | tf_op jit(solution)/shard_map/all_gather | solution.py:75
  69.3 0.1 reshape.114
  69.5 1.6 %fusion.14 = f32[16,96,256]{2,1,0:T(8,128)} fusion(bf16[16,96,32]{1,2,0:T(8,128)(2,1)S(1)} %all-gather, bf16[16,32,256]{2,1,0:T(8,128)(2,1)S(1)} %all-to-all-done.1), kind=kOutput, calls=%fused_computation.23 | convolution fusion | flops 25952256 | bytes 1933312 | tf_op jit(solution)/shard_map/str,src->stc/dot_general | solution.py:79
  71.0 2.1 %reshape.135 = f32[1536,2,128]{2,1,0:T(2,128)S(1)} reshape(f32[16,96,256]{2,1,0:T(8,128)} %fusion.14) | data formatting | bytes 3145728 | tf_op jit(solution)/shard_map/convert_element_type | solution.py:83
  73.1 1.3 %fusion.13 = bf16[2,1536,128]{2,1,0:T(8,128)(2,1)S(1)} fusion(f32[1536,2,128]{2,1,0:T(2,128)S(1)} %reshape.135, bf16[2,1536,128]{2,1,0:T(8,128)(2,1)} %param.19), kind=kLoop, calls=%fused_computation.20 | loop fusion | flops 1179648 | bytes 3145728 | tf_op jit(solution)/shard_map/convert_element_type | solution.py:83
  74.4 4.9 %while.11 = (s32[]{:T(128)}, bf16[2,512,64]{1,2,0:T(8,128)(2,1)S(1)}, bf16[2,512,64]{2,1,0:T(8,128)(2,1)S(1)}, bf16[2,1536,128]{2,1,0:T(8,128)(2,1)S(1)}, s32[16]{0:T(128)S(1)}, /*index=5*/s32[]{:T(128)}) while((s32[]{:T(128)}, bf16[2,512,64]{1,2,0:T(8,128)(2,1)S(1)}, bf16[2,512,64]{2,1,0:T(8,128)(2,1)S(1)}, ...), condition=%wide.region_5.8_spmd.clone, body=%wide.region_2.7_spmd.clone.sunk | while | flops 207651328 | bytes 11223697 | solution.py:88
  74.6 0.7 fusion.71
  75.3 0.6 fusion.72
  75.9 1.0 fusion.73
  77.1 0.7 fusion.71
  77.8 0.6 fusion.72
  78.4 1.0 fusion.73
  79.3 0.2 copy.53
  79.5 0.1 reshape.117
  79.7 0.1 constant_dynamic-slice_fusion
  79.8 0.4 collective-permute-start
  80.2 0.2 collective-permute-start.1
  80.4 1.3 %collective-permute-start.2 = (bf16[1,32,128]{2,1,0:T(8,128)(2,1)S(1)}, bf16[1,32,128]{2,1,0:T(8,128)(2,1)S(1)}, u32[]{:S(2)}, u32[]{:S(2)}) collective-permute-start(bf16[1,32,128]{2,1,0:T(8,128)(2,1)S(1)} %get-tuple-element.105), channel_id=1, source_target_pairs={{0,3},{1,2},{2,1},{3,0},{4,7},{5,6},{6,5},{7,4},{8,11},{9,10},{10,... | collective-permute-start | bytes 24584 | tf_op jit(solution)/shard_map/ppermute | solution.py:100
  81.7 2.0 %collective-permute-start.4 = (bf16[1,32,128]{2,1,0:T(8,128)(2,1)S(1)}, bf16[1,32,128]{2,1,0:T(8,128)(2,1)S(1)}, u32[]{:S(2)}, u32[]{:S(2)}) collective-permute-start(bf16[1,32,128]{2,1,0:T(8,128)(2,1)S(1)} %get-tuple-element.103), channel_id=1, source_target_pairs={{0,5},{1,4},{2,7},{3,6},{4,1},{5,0},{6,3},{7,2},{8,13},{9,12},{10,... | collective-permute-start | bytes 24584 | tf_op jit(solution)/shard_map/ppermute | solution.py:100
  83.7 0.2 collective-permute-done.1
  83.8 2.3 %collective-permute-start.6 = (bf16[1,32,128]{2,1,0:T(8,128)(2,1)S(1)}, bf16[1,32,128]{2,1,0:T(8,128)(2,1)S(1)}, u32[]{:S(2)}, u32[]{:S(2)}) collective-permute-start(bf16[1,32,128]{2,1,0:T(8,128)(2,1)S(1)} %get-tuple-element.101), channel_id=1, source_target_pairs={{0,7},{1,6},{2,5},{3,4},{4,3},{5,2},{6,1},{7,0},{8,15},{9,14},{10,... | collective-permute-start | bytes 24584 | tf_op jit(solution)/shard_map/ppermute | solution.py:100
  86.1 2.9 %collective-permute-start.8 = (bf16[1,32,128]{2,1,0:T(8,128)(2,1)S(1)}, bf16[1,32,128]{2,1,0:T(8,128)(2,1)S(1)}, u32[]{:S(2)}, u32[]{:S(2)}) collective-permute-start(bf16[1,32,128]{2,1,0:T(8,128)(2,1)S(1)} %get-tuple-element.99), channel_id=1, source_target_pairs={{0,9},{1,8},{2,11},{3,10},{4,13},{5,12},{6,15},{7,14},{8,1},{9,0},... | collective-permute-start | bytes 24584 | tf_op jit(solution)/shard_map/ppermute | solution.py:100
  89.1 3.2 %collective-permute-start.10 = (bf16[1,32,128]{2,1,0:T(8,128)(2,1)S(1)}, bf16[1,32,128]{2,1,0:T(8,128)(2,1)S(1)}, u32[]{:S(2)}, u32[]{:S(2)}) collective-permute-start(bf16[1,32,128]{2,1,0:T(8,128)(2,1)S(1)} %get-tuple-element.97), channel_id=1, source_target_pairs={{0,11},{1,10},{2,9},{3,8},{4,15},{5,14},{6,13},{7,12},{8,3},{9,2},... | collective-permute-start | bytes 24584 | tf_op jit(solution)/shard_map/ppermute | solution.py:100
  92.3 3.8 %collective-permute-start.12 = (bf16[1,32,128]{2,1,0:T(8,128)(2,1)S(1)}, bf16[1,32,128]{2,1,0:T(8,128)(2,1)S(1)}, u32[]{:S(2)}, u32[]{:S(2)}) collective-permute-start(bf16[1,32,128]{2,1,0:T(8,128)(2,1)S(1)} %get-tuple-element.95), channel_id=1, source_target_pairs={{0,13},{1,12},{2,15},{3,14},{4,9},{5,8},{6,11},{7,10},{8,5},{9,4},... | collective-permute-start | bytes 24584 | tf_op jit(solution)/shard_map/ppermute | solution.py:100
  96.1 0.2 collective-permute-start.13
  96.3 4.0 %collective-permute-start.14 = (bf16[1,32,128]{2,1,0:T(8,128)(2,1)S(1)}, bf16[1,32,128]{2,1,0:T(8,128)(2,1)S(1)}, u32[]{:S(2)}, u32[]{:S(2)}) collective-permute-start(bf16[1,32,128]{2,1,0:T(8,128)(2,1)S(1)} %get-tuple-element.93), channel_id=1, source_target_pairs={{0,15},{1,14},{2,13},{3,12},{4,11},{5,10},{6,9},{7,8},{8,7},{9,6},... | collective-permute-start | bytes 24584 | tf_op jit(solution)/shard_map/ppermute | solution.py:100
  100.4 0.1 dynamic_update_slice.71
  100.8 1.7 %collective-permute-done.13 = bf16[1,32,128]{2,1,0:T(8,128)(2,1)S(1)} collective-permute-done((bf16[1,32,128]{2,1,0:T(8,128)(2,1)S(1)}, bf16[1,32,128]{2,1,0:T(8,128)(2,1)S(1)}, u32[]{:S(2)}, u32[]{:S(2)}) %collective-permute-start.13) | collective-permute-done | bytes 8224 | tf_op jit(solution)/shard_map/ppermute | solution.py:100
  102.5 0.1 dynamic_update_slice.72
  102.7 0.1 dynamic_update_slice.74
  102.8 0.1 dynamic_update_slice.75
  103.2 0.1 dynamic_update_slice.80
  103.3 0.1 dynamic_update_slice.81
  103.9 4.6 %convolution_convert_fusion.1 = bf16[32,1536]{1,0:T(8,128)(2,1)} fusion(bf16[2048,1536]{1,0:T(8,128)(2,1)} %param.20, bf16[4,8,16,128]{3,2,1,0:T(8,128)(2,1)S(1)} %bitcast.127), kind=kOutput, calls=%fused_computation.18 | convolution fusion | flops 201375744 | bytes 6520832 | tf_op jit(solution)/shard_map/dot_general | solution.py:104
  (69 shorter events, 2.1 us)
Async XLA Ops:
  0.0 11.6 %copy-start = (f32[4096,32]{0,1:T(8,128)S(1)}, f32[4096,32]{0,1:T(8,128)}, u32[]{:S(2)}) copy-start(f32[4096,32]{0,1:T(8,128)} %param.18) | copy-start | bytes 1572868
  1.7 39.1 %all-to-all-start = ((bf16[16,32,128]{2,1,0:T(8,128)(2,1)}), bf16[16,32,128]{2,1,0:T(8,128)(2,1)S(1)}, u32[]{:S(2)}, u32[]{:S(2)}) async-start(bf16[16,32,128]{2,1,0:T(8,128)(2,1)} %bitcast.118), calls=%async_computation | async-start | bytes 262144 | tf_op jit(solution)/shard_map/all_to_all | solution.py:74
  40.8 28.7 %all-to-all-start.1 = ((bf16[16,32,256]{2,1,0:T(8,128)(2,1)}), bf16[16,32,256]{2,1,0:T(8,128)(2,1)S(1)}, u32[]{:S(2)}, u32[]{:S(2)}) async-start(bf16[16,32,256]{2,1,0:T(8,128)(2,1)} %bitcast.117), calls=%async_computation.1 | async-start | bytes 524288 | tf_op jit(solution)/shard_map/all_to_all | solution.py:78
  73.1 1.3 %copy-start.1 = (s32[16]{0:T(128)S(1)}, s32[16]{0:T(128)}, u32[]{:S(2)}) copy-start(s32[16]{0:T(128)} %param.17) | copy-start | bytes 196
  79.8 3.9 %collective-permute-start = (bf16[1,32,128]{2,1,0:T(8,128)(2,1)S(1)}, bf16[1,32,128]{2,1,0:T(8,128)(2,1)S(1)}, u32[]{:S(2)}, u32[]{:S(2)}) collective-permute-start(bf16[1,32,128]{2,1,0:T(8,128)(2,1)S(1)} %get-tuple-element.107), channel_id=1, source_target_pairs={{0,1},{1,0},{2,3},{3,2},{4,5},{5,4},{6,7},{7,6},{8,9},{9,8},{10,11... | collective-permute-start | bytes 24584 | tf_op jit(solution)/shard_map/ppermute | solution.py:100
  80.2 3.7 %collective-permute-start.1 = (bf16[1,32,128]{2,1,0:T(8,128)(2,1)S(1)}, bf16[1,32,128]{2,1,0:T(8,128)(2,1)S(1)}, u32[]{:S(2)}, u32[]{:S(2)}) collective-permute-start(bf16[1,32,128]{2,1,0:T(8,128)(2,1)S(1)} %get-tuple-element.106), channel_id=1, source_target_pairs={{0,2},{1,3},{2,0},{3,1},{4,6},{5,7},{6,4},{7,5},{8,10},{9,11},{10,... | collective-permute-start | bytes 24584 | tf_op jit(solution)/shard_map/ppermute | solution.py:100
  80.4 5.7 %collective-permute-start.2 = (bf16[1,32,128]{2,1,0:T(8,128)(2,1)S(1)}, bf16[1,32,128]{2,1,0:T(8,128)(2,1)S(1)}, u32[]{:S(2)}, u32[]{:S(2)}) collective-permute-start(bf16[1,32,128]{2,1,0:T(8,128)(2,1)S(1)} %get-tuple-element.105), channel_id=1, source_target_pairs={{0,3},{1,2},{2,1},{3,0},{4,7},{5,6},{6,5},{7,4},{8,11},{9,10},{10,... | collective-permute-start | bytes 24584 | tf_op jit(solution)/shard_map/ppermute | solution.py:100
  81.7 4.4 %collective-permute-start.3 = (bf16[1,32,128]{2,1,0:T(8,128)(2,1)S(1)}, bf16[1,32,128]{2,1,0:T(8,128)(2,1)S(1)}, u32[]{:S(2)}, u32[]{:S(2)}) collective-permute-start(bf16[1,32,128]{2,1,0:T(8,128)(2,1)S(1)} %get-tuple-element.104), channel_id=1, source_target_pairs={{0,4},{1,5},{2,6},{3,7},{4,0},{5,1},{6,2},{7,3},{8,12},{9,13},{10,... | collective-permute-start | bytes 24584 | tf_op jit(solution)/shard_map/ppermute | solution.py:100
  81.7 7.3 %collective-permute-start.4 = (bf16[1,32,128]{2,1,0:T(8,128)(2,1)S(1)}, bf16[1,32,128]{2,1,0:T(8,128)(2,1)S(1)}, u32[]{:S(2)}, u32[]{:S(2)}) collective-permute-start(bf16[1,32,128]{2,1,0:T(8,128)(2,1)S(1)} %get-tuple-element.103), channel_id=1, source_target_pairs={{0,5},{1,4},{2,7},{3,6},{4,1},{5,0},{6,3},{7,2},{8,13},{9,12},{10,... | collective-permute-start | bytes 24584 | tf_op jit(solution)/shard_map/ppermute | solution.py:100
  83.7 5.4 %collective-permute-start.5 = (bf16[1,32,128]{2,1,0:T(8,128)(2,1)S(1)}, bf16[1,32,128]{2,1,0:T(8,128)(2,1)S(1)}, u32[]{:S(2)}, u32[]{:S(2)}) collective-permute-start(bf16[1,32,128]{2,1,0:T(8,128)(2,1)S(1)} %get-tuple-element.102), channel_id=1, source_target_pairs={{0,6},{1,7},{2,4},{3,5},{4,2},{5,3},{6,0},{7,1},{8,14},{9,15},{10,... | collective-permute-start | bytes 24584 | tf_op jit(solution)/shard_map/ppermute | solution.py:100
  83.8 8.5 %collective-permute-start.6 = (bf16[1,32,128]{2,1,0:T(8,128)(2,1)S(1)}, bf16[1,32,128]{2,1,0:T(8,128)(2,1)S(1)}, u32[]{:S(2)}, u32[]{:S(2)}) collective-permute-start(bf16[1,32,128]{2,1,0:T(8,128)(2,1)S(1)} %get-tuple-element.101), channel_id=1, source_target_pairs={{0,7},{1,6},{2,5},{3,4},{4,3},{5,2},{6,1},{7,0},{8,15},{9,14},{10,... | collective-permute-start | bytes 24584 | tf_op jit(solution)/shard_map/ppermute | solution.py:100
  86.1 6.2 %collective-permute-start.7 = (bf16[1,32,128]{2,1,0:T(8,128)(2,1)S(1)}, bf16[1,32,128]{2,1,0:T(8,128)(2,1)S(1)}, u32[]{:S(2)}, u32[]{:S(2)}) collective-permute-start(bf16[1,32,128]{2,1,0:T(8,128)(2,1)S(1)} %get-tuple-element.100), channel_id=1, source_target_pairs={{0,8},{1,9},{2,10},{3,11},{4,12},{5,13},{6,14},{7,15},{8,0},{9,1},... | collective-permute-start | bytes 24584 | tf_op jit(solution)/shard_map/ppermute | solution.py:100
  86.1 10.0 %collective-permute-start.8 = (bf16[1,32,128]{2,1,0:T(8,128)(2,1)S(1)}, bf16[1,32,128]{2,1,0:T(8,128)(2,1)S(1)}, u32[]{:S(2)}, u32[]{:S(2)}) collective-permute-start(bf16[1,32,128]{2,1,0:T(8,128)(2,1)S(1)} %get-tuple-element.99), channel_id=1, source_target_pairs={{0,9},{1,8},{2,11},{3,10},{4,13},{5,12},{6,15},{7,14},{8,1},{9,0},... | collective-permute-start | bytes 24584 | tf_op jit(solution)/shard_map/ppermute | solution.py:100
  89.0 7.3 %collective-permute-start.9 = (bf16[1,32,128]{2,1,0:T(8,128)(2,1)S(1)}, bf16[1,32,128]{2,1,0:T(8,128)(2,1)S(1)}, u32[]{:S(2)}, u32[]{:S(2)}) collective-permute-start(bf16[1,32,128]{2,1,0:T(8,128)(2,1)S(1)} %get-tuple-element.98), channel_id=1, source_target_pairs={{0,10},{1,11},{2,8},{3,9},{4,14},{5,15},{6,12},{7,13},{8,2},{9,3},... | collective-permute-start | bytes 24584 | tf_op jit(solution)/shard_map/ppermute | solution.py:100
  89.1 11.6 %collective-permute-start.10 = (bf16[1,32,128]{2,1,0:T(8,128)(2,1)S(1)}, bf16[1,32,128]{2,1,0:T(8,128)(2,1)S(1)}, u32[]{:S(2)}, u32[]{:S(2)}) collective-permute-start(bf16[1,32,128]{2,1,0:T(8,128)(2,1)S(1)} %get-tuple-element.97), channel_id=1, source_target_pairs={{0,11},{1,10},{2,9},{3,8},{4,15},{5,14},{6,13},{7,12},{8,3},{9,2},... | collective-permute-start | bytes 24584 | tf_op jit(solution)/shard_map/ppermute | solution.py:100
  92.3 8.4 %collective-permute-start.11 = (bf16[1,32,128]{2,1,0:T(8,128)(2,1)S(1)}, bf16[1,32,128]{2,1,0:T(8,128)(2,1)S(1)}, u32[]{:S(2)}, u32[]{:S(2)}) collective-permute-start(bf16[1,32,128]{2,1,0:T(8,128)(2,1)S(1)} %get-tuple-element.96), channel_id=1, source_target_pairs={{0,12},{1,13},{2,14},{3,15},{4,8},{5,9},{6,10},{7,11},{8,4},{9,5},... | collective-permute-start | bytes 24584 | tf_op jit(solution)/shard_map/ppermute | solution.py:100
  92.3 8.4 %collective-permute-start.12 = (bf16[1,32,128]{2,1,0:T(8,128)(2,1)S(1)}, bf16[1,32,128]{2,1,0:T(8,128)(2,1)S(1)}, u32[]{:S(2)}, u32[]{:S(2)}) collective-permute-start(bf16[1,32,128]{2,1,0:T(8,128)(2,1)S(1)} %get-tuple-element.95), channel_id=1, source_target_pairs={{0,13},{1,12},{2,15},{3,14},{4,9},{5,8},{6,11},{7,10},{8,5},{9,4},... | collective-permute-start | bytes 24584 | tf_op jit(solution)/shard_map/ppermute | solution.py:100
  96.1 6.3 %collective-permute-start.13 = (bf16[1,32,128]{2,1,0:T(8,128)(2,1)S(1)}, bf16[1,32,128]{2,1,0:T(8,128)(2,1)S(1)}, u32[]{:S(2)}, u32[]{:S(2)}) collective-permute-start(bf16[1,32,128]{2,1,0:T(8,128)(2,1)S(1)} %get-tuple-element.94), channel_id=1, source_target_pairs={{0,14},{1,15},{2,12},{3,13},{4,10},{5,11},{6,8},{7,9},{8,6},{9,7},... | collective-permute-start | bytes 24584 | tf_op jit(solution)/shard_map/ppermute | solution.py:100
  96.3 6.2 %collective-permute-start.14 = (bf16[1,32,128]{2,1,0:T(8,128)(2,1)S(1)}, bf16[1,32,128]{2,1,0:T(8,128)(2,1)S(1)}, u32[]{:S(2)}, u32[]{:S(2)}) collective-permute-start(bf16[1,32,128]{2,1,0:T(8,128)(2,1)S(1)} %get-tuple-element.93), channel_id=1, source_target_pairs={{0,15},{1,14},{2,13},{3,12},{4,11},{5,10},{6,9},{7,8},{8,7},{9,6},... | collective-permute-start | bytes 24584 | tf_op jit(solution)/shard_map/ppermute | solution.py:100
